TPU v7x, 32 devices: a whole 2x2x4 slice. The times are simulated.
32 devices in a mesh: dp: 2 (over x), expert: 16 (over z, y, core).
Axes of the slice: x: 2, y: 2, z: 4, core: 2. Of those that a mesh axis runs over, the one named last changes fastest.
Arguments:
- tokens: bfloat16 [8192, 1024], P(('dp', 'expert')), may hold values from -6 to 6
- modulation: bfloat16 [32, 2, 1024], P(('dp', 'expert')), may hold values from -3 to 3
- router_weight: bfloat16 [1024, 16], replicated, may hold values from -0.1875 to 0.1875
- weight_in: bfloat16 [16, 1024, 4096], P('expert', None, 'dp'), may hold values from -0.1875 to 0.1875
- weight_out: bfloat16 [16, 4096, 1024], P('expert', 'dp'), may hold values from -0.09375 to 0.09375
- chosen: int32 [2, 16, 256], P('dp'), may hold values from 0 to 4095, as said below
- grad_out: bfloat16 [8192, 1024], P(('dp', 'expert')), may hold values from -4 to 4
Outputs:
- grad_tokens: bfloat16 [8192, 1024], P(('dp', 'expert'))
- grad_mod: float32 [32, 2, 1024], P(('dp', 'expert'))
- grad_router: float32 [1024, 16], replicated
- grad_weight_in: bfloat16 [16, 1024, 4096], P('expert', None, 'dp')
- grad_weight_out: bfloat16 [16, 4096, 1024], P('expert', 'dp')
Inputs may be any that keep to these rules, and one draw needn't show every extreme that they name: `chosen`: for each slice and expert the 256 positions are distinct; at most 32 of them lie in one image's 256 tokens, and in one image exactly 32.
All inputs are finite; a program needn't handle non-finite values.
Results may differ from a plain program's by a relative error of at most 0.008.
Values may be sent and summed in bfloat16 or wider, within the bound.
No kernel may reach another device: no remote copies, remote signals or barrier semaphores. Data moves between devices by JAX's collectives and lax.ppermute only.
A program may use at most 128 MiB of HBM per device.

v0:
```python
import jax
import jax.numpy as jnp
from jax import lax
from jax.sharding import PartitionSpec as P

gelu_root = 0.7978845608028654
gelu_cube = 0.044715
norm_eps = 1e-06


def gelu_value(values):
    inner = gelu_root * (values + gelu_cube * values * values * values)
    return 0.5 * values * (1.0 + jnp.tanh(inner))


def gelu_slope(values):
    tangent = jnp.tanh(gelu_root * (values + gelu_cube * values * values * values))
    return 0.5 * (1.0 + tangent) + 0.5 * values * (1.0 - tangent * tangent) * gelu_root * (
        1.0 + 3.0 * gelu_cube * values * values
    )


def finish_terms(preact, upstream, rows_g, rows_p):
    hidden = gelu_value(preact).astype(jnp.bfloat16)
    score_sum = jnp.sum(hidden.astype(jnp.float32) * upstream, axis=1)
    prob_col = rows_p.astype(jnp.float32)[:, None]
    grad_y = (prob_col * rows_g.astype(jnp.float32)).astype(jnp.bfloat16)
    grad_pre = (prob_col * upstream * gelu_slope(preact)).astype(jnp.bfloat16)
    return (hidden, score_sum, grad_y, grad_pre)


def body(tokens, modulation, router_weight, weight_in, weight_out, chosen, grad_out):
    tok_count = tokens.shape[0]
    model_width = tokens.shape[1]
    experts = lax.axis_size("expert")
    my_index = lax.axis_index("expert")
    most_rows = 2 * tok_count // experts
    x_float = tokens.astype(jnp.float32)
    average = jnp.mean(x_float, axis=1, keepdims=True)
    centred = x_float - average
    spread = jnp.mean(centred * centred, axis=1, keepdims=True)
    inverse = lax.rsqrt(spread + norm_eps)
    normed = centred * inverse
    shift_mod = modulation[0, 0].astype(jnp.float32)
    scale_mod = modulation[0, 1].astype(jnp.float32)
    normal_u = (normed * (1.0 + scale_mod) + shift_mod).astype(jnp.bfloat16)
    gate_prob = jax.nn.sigmoid(
        jnp.dot(normal_u, router_weight, preferred_element_type=jnp.float32)
    ).astype(jnp.bfloat16)
    picked = chosen[0]
    local_row = picked - my_index * tok_count
    is_mine = (local_row >= 0) & (local_row < tok_count)
    rank_in = jnp.cumsum(is_mine.astype(jnp.int32), axis=1) - 1
    slot_at = jnp.where(is_mine, rank_in, most_rows)
    expert_col = jnp.arange(experts, dtype=jnp.int32)[:, None]
    rows_idx = (
        jnp.full((experts, most_rows), tok_count, jnp.int32)
        .at[expert_col, slot_at]
        .set(local_row, mode="drop")
    )
    u_pad = jnp.concatenate([normal_u, jnp.zeros((1, model_width), jnp.bfloat16)], axis=0)
    g_pad = jnp.concatenate([grad_out, jnp.zeros((1, model_width), jnp.bfloat16)], axis=0)
    p_pad = jnp.concatenate([gate_prob, jnp.zeros((1, experts), jnp.bfloat16)], axis=0)
    u_send = u_pad[rows_idx]
    g_send = g_pad[rows_idx]
    p_send = p_pad[rows_idx, expert_col]
    u_recv, g_recv, p_recv = (
        lax.all_to_all(u_send, "expert", split_axis=0, concat_axis=0, tiled=True),
        lax.all_to_all(g_send, "expert", split_axis=0, concat_axis=0, tiled=True),
        lax.all_to_all(p_send, "expert", split_axis=0, concat_axis=0, tiled=True),
    )
    u_all, g_all, p_all = (
        lax.all_gather(u_recv, "dp", axis=0, tiled=True),
        lax.all_gather(g_recv, "dp", axis=0, tiled=True),
        lax.all_gather(p_recv, "dp", axis=0, tiled=True),
    )
    rows_u = u_all.reshape(-1, model_width)
    rows_g = g_all.reshape(-1, model_width)
    rows_p = p_all.reshape(-1)
    first_w = weight_in[0]
    second_w = weight_out[0]
    preact = jnp.dot(rows_u, first_w, preferred_element_type=jnp.float32)
    upstream = lax.dot_general(
        rows_g, second_w, (((1,), (1,)), ((), ())), preferred_element_type=jnp.float32
    )
    hidden, score_sum, grad_y, grad_pre = finish_terms(preact, upstream, rows_g, rows_p)
    grad_first = lax.dot_general(
        rows_u, grad_pre, (((0,), (0,)), ((), ())), preferred_element_type=jnp.float32
    )
    grad_second = lax.dot_general(
        hidden, grad_y, (((0,), (0,)), ((), ())), preferred_element_type=jnp.float32
    )
    rows_part = lax.dot_general(
        grad_pre, first_w, (((1,), (1,)), ((), ())), preferred_element_type=jnp.float32
    )
    grad_sum, score_total = (
        lax.psum_scatter(
            rows_part.reshape(-1, most_rows, model_width), "dp", scatter_dimension=0, tiled=True
        ),
        lax.psum_scatter(score_sum.reshape(-1, most_rows), "dp", scatter_dimension=0, tiled=True),
    )
    grad_weight_in = grad_first.astype(jnp.bfloat16)[None]
    grad_weight_out = grad_second.astype(jnp.bfloat16)[None]
    grad_back = grad_sum.astype(jnp.bfloat16)
    score_back = score_total.astype(jnp.bfloat16)
    prob_recv = p_recv.astype(jnp.float32)
    logit_slots = score_back.astype(jnp.float32) * prob_recv * (1.0 - prob_recv)
    column = jnp.sum(u_recv.astype(jnp.float32) * logit_slots[:, :, None], axis=(0, 1))
    column = lax.psum(column, "dp")
    grad_router = lax.all_gather(column[:, None], "expert", axis=1, tiled=True)
    grad_ret, score_ret = (
        lax.all_to_all(grad_back, "expert", split_axis=0, concat_axis=0, tiled=True),
        lax.all_to_all(score_back, "expert", split_axis=0, concat_axis=0, tiled=True),
    )
    grad_u = (
        jnp.zeros((tok_count + 1, model_width), jnp.float32)
        .at[rows_idx]
        .add(grad_ret.astype(jnp.float32))[:tok_count]
    )
    prob_sent = p_send.astype(jnp.float32)
    logit_terms = score_ret.astype(jnp.float32) * prob_sent * (1.0 - prob_sent)
    grad_logit = (
        jnp.zeros((tok_count + 1, experts), jnp.float32)
        .at[rows_idx, expert_col]
        .add(logit_terms)[:tok_count]
    )
    grad_u = grad_u + jnp.dot(
        grad_logit, router_weight.astype(jnp.float32).T, precision=lax.Precision.HIGHEST
    )
    grad_shift = jnp.sum(grad_u, axis=0)
    grad_scale = jnp.sum(grad_u * normed, axis=0)
    grad_mod = jnp.stack([grad_shift, grad_scale], axis=0)[None]
    grad_norm = grad_u * (1.0 + scale_mod)
    centre_term = jnp.mean(grad_norm, axis=1, keepdims=True)
    slope_term = jnp.mean(grad_norm * normed, axis=1, keepdims=True)
    grad_tokens = (
        grad_out.astype(jnp.float32) + (grad_norm - centre_term - normed * slope_term) * inverse
    ).astype(jnp.bfloat16)
    return (grad_tokens, grad_mod, grad_router, grad_weight_in, grad_weight_out)


def solution(mesh):
    placed = (
        P(("dp", "expert"), None),
        P(("dp", "expert"), None, None),
        P(),
        P("expert", None, "dp"),
        P("expert", "dp", None),
        P("dp", None, None),
        P(("dp", "expert"), None),
    )
    return jax.shard_map(
        body,
        mesh=mesh,
        in_specs=placed,
        out_specs=(
            P(("dp", "expert"), None),
            P(("dp", "expert"), None, None),
            P(),
            P("expert", None, "dp"),
            P("expert", "dp", None),
        ),
        check_vma=False,
    )
```

profile of v0, /device:TPU:0, one launch (start us, length us, event | category | flops | bytes accessed | tf_op | source)
XLA Modules:
  0.0 315.4 jit_solution(3350218393936861215)
XLA Ops:
  7.2 0.7 slice_convert_fusion
  7.9 0.7 convert_add_fusion
  8.6 0.7 subtract_bitcast_fusion
  9.3 0.7 fusion.44
  10.1 1.2 convert_reduce_fusion
  11.3 1.3 fusion.34
  12.6 0.6 reduce-window.6
  13.2 0.2 slice_reduce_fusion
  13.6 0.7 and_reduce_fusion
  14.3 0.7 multiply_reduce_fusion.3
  15.1 15.5 %scatter_custom_fusion.2 = s32[512]{0:T(512)S(1)} fusion(s32[4096]{0:T(1024)S(1)} %bitcast.85, s32[4096]{0:T(1024)S(1)} %bitcast.84, s32[]{:T(128)} %constant.16.clone.1), kind=kCustom, calls=%fused_computation.83 | custom fusion | bytes 2052
  30.7 0.1 reshape.193
  30.8 1.3 fusion.27
  32.2 2.1 gather_fusion.2
  34.2 32.0 %all_to_all.37 = bf16[16,32,1024]{2,1,0:T(8,128)(2,1)} all-to-all(bf16[16,32,1024]{2,1,0:T(8,128)(2,1)S(1)} %bitcast.75), channel_id=1, replica_groups=mesh['dp'=2,'expert'=16] {'expert'}, dimensions={0} | all-to-all | bytes 2097152 | tf_op jit(solution)/shard_map/all_to_all | solution.py:68
  66.4 2.1 gather_fusion.1
  68.4 29.6 %all_to_all.38 = bf16[16,32,1024]{2,1,0:T(8,128)(2,1)} all-to-all(bf16[16,32,1024]{2,1,0:T(8,128)(2,1)S(1)} %bitcast.74), channel_id=1, replica_groups=mesh['dp'=2,'expert'=16] {'expert'}, dimensions={0} | all-to-all | bytes 2097152 | tf_op jit(solution)/shard_map/all_to_all | solution.py:69
  98.1 0.1 reshape.169
  98.2 0.3 fusion.25
  98.5 4.9 %gather_fusion = bf16[512]{0:T(512)(128)(2,1)S(1)} fusion(bf16[257,16]{0,1:T(8,128)(2,1)S(1)} %concatenate.17, s32[512]{0:T(512)S(1)} %reshape.169), kind=kCustom, calls=%fused_computation | custom fusion | bytes 6144 | tf_op jit(solution)/shard_map/gather | solution.py:66
  103.4 0.1 all_to_all.31
  103.5 11.3 %all_to_all.39 = bf16[16,1,32]{2,1,0:T(2,128)(2,1)S(1)} all-to-all(bf16[16,1,32]{2,1,0:T(2,128)(2,1)S(1)} %all_to_all.31), channel_id=1, replica_groups=mesh['dp'=2,'expert'=16] {'expert'}, dimensions={0} | all-to-all | bytes 2048 | tf_op jit(solution)/shard_map/all_to_all | solution.py:70
  114.8 4.7 %all-gather = bf16[32,1,32]{2,0,1:T(8,128)(2,1)S(1)} all-gather(bf16[16,1,32]{2,0,1:T(8,128)(2,1)S(1)} %copy.27), channel_id=2, replica_groups=mesh['dp'=2,'expert'=16] {'dp'}, dimensions={0}, use_global_device_ids=true | all-gather | bytes 3072 | tf_op jit(solution)/shard_map/all_gather | solution.py:75
  119.5 0.1 reshape.167
  119.6 10.5 %fusion.9 = f32[1024,2048]{1,0:T(8,128)} fusion(bf16[1024,1024]{1,0:T(8,128)(2,1)} %bitcast.88, bf16[1,1024,2048]{2,1,0:T(8,128)(2,1)} %param.10), kind=kOutput, calls=%fused_computation.19 | convolution fusion | flops 4294967296 | bytes 14680064 | tf_op jit(solution)/shard_map/dot_general | solution.py:82
  130.1 4.5 %all-gather.5.cloned.1.call-done = bf16[32,32,1024]{2,1,0:T(8,128)(2,1)} async-done(((bf16[16,32,1024]{2,1,0:T(8,128)(2,1)}), bf16[32,32,1024]{2,1,0:T(8,128)(2,1)}) %all-gather.5.cloned.1.call-update) | async-done | bytes 2097168 | tf_op jit(solution)/shard_map/all_gather | solution.py:74
  134.6 14.5 %multiply_reduce_fusion = (f32[1024]{0:T(1024)S(1)}, bf16[1024,2048]{1,0:T(8,128)(2,1)}) fusion(f32[1024,2048]{1,0:T(8,128)} %fusion.9, f32[1024]{0:T(1024)S(1)} %reshape.167, bf16[1024,1024]{1,0:T(8,128)(2,1)} %bitcast.90, bf16[1,2048,1024]{2,1,0:T(8,128)(2,1)} %param.11), kind=kOutput, calls=%fused_computation.15 | convolution fusion | flops 4347395072 | bytes 18882560 | tf_op jit(solution)/shard_map/dot_general | solution.py:83
  149.1 0.7 reshape.160
  149.9 10.0 %fusion.7 = f32[32,32,1024]{2,1,0:T(8,128)} fusion(bf16[32,32,2048]{2,1,0:T(8,128)(2,1)} %bitcast.92, bf16[1,1024,2048]{2,1,0:T(8,128)(2,1)} %param.10), kind=kOutput, calls=%fused_computation.17 | convolution fusion | flops 4294967296 | bytes 12582912 | tf_op jit(solution)/shard_map/dot_general | solution.py:93
  160.0 0.7 subtract_multiply_fusion
  160.7 0.6 copy.28
  161.3 5.6 %all-to-all-start.4 = ((bf16[16,1,32]{2,1,0:T(2,128)(2,1)}), bf16[16,1,32]{2,1,0:T(2,128)(2,1)S(1)}, u32[]{:S(2)}, u32[]{:S(2)}) async-start(bf16[16,1,32]{2,1,0:T(2,128)(2,1)} %copy.28), calls=%async_computation.6 | async-start | bytes 16384 | tf_op jit(solution)/shard_map/all_to_all | solution.py:113
  166.9 0.1 reshape.223
  167.1 50.0 %reduce-scatter.3.cloned.1.call-done = f32[16,32,1024]{2,1,0:T(8,128)} async-done(((f32[32,32,1024]{2,1,0:T(8,128)}), f32[16,32,1024]{2,1,0:T(8,128)}) %reduce-scatter.3.cloned.1.call-update) | async-done | bytes 2097168 | tf_op jit(solution)/shard_map/reduce_scatter | solution.py:97
  217.1 2.8 convert_element_type.111
  219.8 5.6 %all-to-all-start.3 = ((bf16[16,32,1024]{2,1,0:T(8,128)(2,1)}), bf16[16,32,1024]{2,1,0:T(8,128)(2,1)S(1)}, u32[]{:S(2)}, u32[]{:S(2)}) async-start(bf16[16,32,1024]{2,1,0:T(8,128)(2,1)} %convert_element_type.111), calls=%async_computation.4 | async-start | bytes 2097152 | tf_op jit(solution)/shard_map/all_to_all | solution.py:112
  225.5 9.6 %convert_bitcast_fusion.1 = bf16[1,1024,2048]{2,1,0:T(8,128)(2,1)} fusion(bf16[1024,1024]{1,0:T(8,128)(2,1)} %bitcast.89, bf16[1024,2048]{1,0:T(8,128)(2,1)} %get-tuple-element.12), kind=kOutput, calls=%fused_computation.25 | convolution fusion | flops 4297064448 | bytes 10485760 | tf_op jit(solution)/shard_map/dot_general | solution.py:87
  235.0 11.7 %convert_bitcast_fusion = bf16[1,2048,1024]{2,1,0:T(8,128)(2,1)} fusion(bf16[1024,1024]{1,0:T(8,128)(2,1)S(1)} %bitcast.91, f32[1024]{0:T(1024)S(1)} %reshape.167, f32[1024,2048]{1,0:T(8,128)} %fusion.9), kind=kOutput, calls=%fused_computation.23 | convolution fusion | flops 4319084544 | bytes 14684160 | tf_op jit(solution)/shard_map/dot_general | solution.py:90
  246.7 0.3 multiply_reduce_fusion.1
  247.0 4.9 %psum.7 = f32[1024,1]{0,1:T(1,128)S(1)} all-reduce(f32[1024,1]{0,1:T(1,128)S(1)} %bitcast.82), channel_id=1, replica_groups=mesh['dp'=2,'expert'=16] {'dp'}, use_global_device_ids=true, to_apply=%region_15.16 | all-reduce | flops 1024 | bytes 8192 | tf_op jit(solution)/shard_map/psum | solution.py:109
  252.0 22.1 %all-gather.1 = f32[16,1,1024]{2,1,0:T(1,128)S(1)} all-gather(f32[1,1,1024]{2,1,0:T(1,128)S(1)} %bitcast.83), channel_id=1, replica_groups=mesh['dp'=2,'expert'=16] {'expert'}, dimensions={0}, use_global_device_ids=true | all-gather | bytes 69632 | tf_op jit(solution)/shard_map/all_gather | solution.py:110
  274.1 0.6 copy.35
  274.7 0.1 reshape.201
  274.8 25.9 %scatter_fusion = f32[257,16]{0,1:T(8,128)S(1)} fusion(f32[257,16]{0,1:T(8,128)S(1)} %broadcast_in_dim.30, s32[512]{0:T(512)S(1)} %reshape.199, f32[512]{0:T(512)S(1)} %reshape.201), kind=kCustom, calls=%fused_computation.4 | custom fusion | flops 512 | bytes 10240 | tf_op jit(solution)/shard_map/scatter-add | solution.py:125
  300.7 5.1 %scatter_custom_fusion = f32[257,1024]{1,0:T(8,128)S(1)} fusion(s32[512]{0:T(512)S(1)} %reshape.193, bf16[512,1024]{1,0:T(8,128)(2,1)S(1)} %bitcast.73, f32[]{:T(128)} %constant.15.clone.1), kind=kCustom, calls=%fused_computation.26 | custom fusion | flops 1048576 | bytes 2101252 | tf_op jit(solution)/shard_map/scatter-add | solution.py:118
  305.8 1.1 fusion.33
  307.0 0.6 maximum_bitcast_fusion
  307.6 1.3 fusion.32
  (49 shorter events, 0.8 us)
Async XLA Ops:
  7.2 91.0 %copy-start = (bf16[1024,16]{0,1:T(8,128)(2,1)S(1)}, bf16[1024,16]{0,1:T(8,128)(2,1)}, u32[]{:S(2)}) copy-start(bf16[1024,16]{0,1:T(8,128)(2,1)} %param.9) | copy-start | bytes 98308
  7.2 112.4 %all-gather.7.cloned.1.call-start = ((), (), s32[]{:S(2)}) async-start(), calls=%async_computation.8 | async-start | bytes 3145728 | tf_op jit(solution)/shard_map/all_gather | solution.py:73
  32.1 34.2 %copy-start.3 = (bf16[256,1024]{1,0:T(8,128)(2,1)S(1)}, bf16[256,1024]{1,0:T(8,128)(2,1)}, u32[]{:S(2)}) copy-start(bf16[256,1024]{1,0:T(8,128)(2,1)} %param.13) | copy-start | bytes 1572868
  66.3 68.4 %all-gather.5.cloned.1.call-start = ((), (), s32[]{:S(2)}) async-start(), calls=%async_computation.7 | async-start | bytes 3145728 | tf_op jit(solution)/shard_map/all_gather | solution.py:74
  98.1 61.9 %reduce-scatter.5.cloned.1.call-start = ((), (), s32[]{:S(2)}) async-start(), calls=%async_computation.10 | async-start | bytes 24576 | tf_op jit(solution)/shard_map/reduce_scatter | solution.py:100
  149.8 67.2 %reduce-scatter.3.cloned.1.call-start = ((), (), s32[]{:S(2)}) async-start(), calls=%async_computation.9 | async-start | bytes 6291456 | tf_op jit(solution)/shard_map/reduce_scatter | solution.py:97
  161.3 58.6 %all-to-all-start.4 = ((bf16[16,1,32]{2,1,0:T(2,128)(2,1)}), bf16[16,1,32]{2,1,0:T(2,128)(2,1)S(1)}, u32[]{:S(2)}, u32[]{:S(2)}) async-start(bf16[16,1,32]{2,1,0:T(2,128)(2,1)} %copy.28), calls=%async_computation.6 | async-start | bytes 16384 | tf_op jit(solution)/shard_map/all_to_all | solution.py:113
  219.8 80.9 %all-to-all-start.3 = ((bf16[16,32,1024]{2,1,0:T(8,128)(2,1)}), bf16[16,32,1024]{2,1,0:T(8,128)(2,1)S(1)}, u32[]{:S(2)}, u32[]{:S(2)}) async-start(bf16[16,32,1024]{2,1,0:T(8,128)(2,1)} %convert_element_type.111), calls=%async_computation.4 | async-start | bytes 2097152 | tf_op jit(solution)/shard_map/all_to_all | solution.py:112
  225.5 9.6 %copy-start.4 = (bf16[32,32,1024]{2,1,0:T(8,128)(2,1)S(1)}, bf16[32,32,1024]{2,1,0:T(8,128)(2,1)}, u32[]{:S(2)}) copy-start(bf16[32,32,1024]{2,1,0:T(8,128)(2,1)} %all-gather.5.cloned.1.call-done) | copy-start | bytes 6291460
  235.0 11.7 %copy-start.1 = (bf16[16,32,1024]{2,1,0:T(8,128)(2,1)S(1)}, bf16[16,32,1024]{2,1,0:T(8,128)(2,1)}, u32[]{:S(2)}) copy-start(bf16[16,32,1024]{2,1,0:T(8,128)(2,1)} %all_to_all.37) | copy-start | bytes 3145732
  274.8 31.0 %copy-start.2 = (bf16[256,1024]{1,0:T(8,128)(2,1)S(1)}, bf16[256,1024]{1,0:T(8,128)(2,1)}, u32[]{:S(2)}) copy-start(bf16[256,1024]{1,0:T(8,128)(2,1)} %param.7) | copy-start | bytes 1572868
Sparse Core Ops, SparseCore 0:
  66.4 33.4 all-gather.6
  101.4 33.1 all-gather.4
  150.0 9.9 reduce-scatter.4
  162.7 54.3 reduce-scatter.2
where the time goes:
time: 316 us; the launch traced here: 315 us
  blocking collectives  105 us (33%)
  matrix products  57.7 us (18%)
  waiting for transfers between devices  54.6 us (17%)
  other arithmetic  45.5 us (14%)
  local copies, waits for them, and re-layouts  27.5 us (9%)
  between operations  14 us (4%)
  starting transfers between devices  11.4 us (4%)
    reduce_scatter x1, waiting for transfers between devices, body(): lax.psum_scatter(rows_part.reshape(-1, most_rows, model_width), 'dp', sca...  50 us
    all_to_all x1, blocking collectives, body(): lax.all_to_all(u_send, 'expert', split_axis=0, concat_axis=0, tiled=True)  32 us
    all_to_all x1, blocking collectives, body(): lax.all_to_all(g_send, 'expert', split_axis=0, concat_axis=0, tiled=True)  29.6 us
    scatter-add x1, other arithmetic, body(): grad_logit = jnp.zeros((tok_count + 1, experts), jnp.float32).at[rows_idx...  25.9 us
    all_gather x1, blocking collectives, body(): grad_router = lax.all_gather(column[:, None], 'expert', axis=1, tiled=True)  22.1 us
    unnamed x14, local copies, waits for them, and re-layouts  16.2 us
    dot_general x1, matrix products, body(): lax.dot_general(rows_g, second_w, (((1,), (1,)), ((), ())), preferred_ele...  14.5 us
    dot_general x1, matrix products, body(): lax.dot_general(hidden, grad_y, (((0,), (0,)), ((), ())), preferred_eleme...  11.7 us
  transfers between devices with their start and end apart: 6, of which 2 were waited for; matrix products, arithmetic and copies ran while one was open for 25% of the time, Pallas kernels for 0%

commit v1 on v0

--- a/solution.py
+++ b/solution.py
@@ -1,11 +1,34 @@
+import functools
 import jax
 import jax.numpy as jnp
 from jax import lax
 from jax.sharding import PartitionSpec as P
+from jax.lax import axis_index, axis_size, ppermute
 
 gelu_root = 0.7978845608028654
 gelu_cube = 0.044715
 norm_eps = 1e-06
+
+
+def _define_kinds(inputs, dev_axis):
+    n_blocks = axis_size(dev_axis)
+    line_up = [(pp, (pp + 1) % n_blocks) for pp in range(n_blocks)]
+    seen = [(pp, (pp - 1) % n_blocks) for pp in range(n_blocks)]
+    ready, reached = ([inputs], [inputs])
+    for _ in range(n_blocks // 2):
+        ready.append(ppermute(ready[-1], dev_axis, line_up))
+    q = 0
+    while q < (n_blocks - 1) // 2:
+        reached.append(ppermute(reached[-1], axis_name=dev_axis, perm=seen))
+        q += 1
+    return jnp.roll(
+        jnp.concatenate([*ready[::-1], *reached[1:]], axis=1),
+        (axis_index(dev_axis) - n_blocks // 2) * inputs.shape[1],
+        axis=1,
+    )
+
+
+_follow_point = functools.partial(_define_kinds, dev_axis="expert")
 
 
 def gelu_value(values):
@@ -107,7 +130,7 @@
     logit_slots = score_back.astype(jnp.float32) * prob_recv * (1.0 - prob_recv)
     column = jnp.sum(u_recv.astype(jnp.float32) * logit_slots[:, :, None], axis=(0, 1))
     column = lax.psum(column, "dp")
-    grad_router = lax.all_gather(column[:, None], "expert", axis=1, tiled=True)
+    grad_router = _follow_point(column[:, None])
     grad_ret, score_ret = (
         lax.all_to_all(grad_back, "expert", split_axis=0, concat_axis=0, tiled=True),
         lax.all_to_all(score_back, "expert", split_axis=0, concat_axis=0, tiled=True),

time: 316 us -> 295 us (0.934)
  starting transfers between devices: 11.4 us -> 42.4 us
  waiting for transfers between devices: 54.6 us -> 26.7 us
  blocking collectives: 105 us -> 82.5 us
    reduce_scatter x1, waiting for transfers between devices: 50 us -> 16.8 us  [body(): lax.psum_scatter(rows_part.reshape(-1, most_rows, model_width), 'dp', sca...]
    ppermute x0 -> x15, starting transfers between devices: none -> 30.8 us  [the longest x7 30.7 us: _define_kinds(): reached.append(ppermute(reached[-1], axis_name=dev_axis, perm=seen))]
    all_gather x1 -> x0, blocking collectives: 22.1 us -> none  [body(): grad_router = lax.all_gather(column[:, None], 'expert', axis=1, tiled=True)]
    ppermute x0 -> x15, waiting for transfers between devices: none -> 5.28 us  [the longest x8 5.14 us: _define_kinds(): ready.append(ppermute(ready[-1], dev_axis, line_up))]
    dot_general x1, matrix products: 9.56 us -> 6.12 us  [body(): lax.dot_general(rows_u, grad_pre, (((0,), (0,)), ((), ())), preferred_ele...]
    unnamed x14 -> x15, local copies, waits for them, and re-layouts: 16.2 us -> 15.9 us
  transfers between devices with their start and end apart: 6 -> 21, of which waited for: 2 -> 6; matrix products, arithmetic and copies ran while one was open for 25% -> 26% of each run, Pallas kernels for 0% -> 0%
where the time goes in v1:
time: 295 us; the launch traced here: 294 us
  blocking collectives  82.5 us (28%)
  matrix products  54.9 us (19%)
  other arithmetic  45.5 us (15%)
  starting transfers between devices  42.4 us (14%)
  local copies, waits for them, and re-layouts  28.1 us (10%)
  waiting for transfers between devices  26.7 us (9%)
  between operations  14.1 us (5%)
    all_to_all x1, blocking collectives, body(): lax.all_to_all(u_send, 'expert', split_axis=0, concat_axis=0, tiled=True)  32 us
    ppermute x7, starting transfers between devices, _define_kinds(): reached.append(ppermute(reached[-1], axis_name=dev_axis, perm=seen))  30.7 us
    all_to_all x1, blocking collectives, body(): lax.all_to_all(g_send, 'expert', split_axis=0, concat_axis=0, tiled=True)  29.6 us
    scatter-add x1, other arithmetic, body(): grad_logit = jnp.zeros((tok_count + 1, experts), jnp.float32).at[rows_idx...  25.9 us
    reduce_scatter x1, waiting for transfers between devices, body(): lax.psum_scatter(rows_part.reshape(-1, most_rows, model_width), 'dp', sca...  16.8 us
    unnamed x15, local copies, waits for them, and re-layouts  15.9 us
    dot_general x1, matrix products, body(): lax.dot_general(rows_g, second_w, (((1,), (1,)), ((), ())), preferred_ele...  14.5 us
    dot_general x1, matrix products, body(): lax.dot_general(hidden, grad_y, (((0,), (0,)), ((), ())), preferred_eleme...  12.4 us
  transfers between devices with their start and end apart: 21, of which 6 were waited for; matrix products, arithmetic and copies ran while one was open for 26% of the time, Pallas kernels for 0%

profile of v1, /device:TPU:0, one launch (start us, length us, event | category | flops | bytes accessed | tf_op | source)
XLA Modules:
  0.0 294.3 jit_solution(7245434862311014210)
XLA Ops:
  7.2 0.7 slice_convert_fusion
  7.9 0.7 convert_add_fusion
  8.6 0.7 subtract_bitcast_fusion
  9.3 0.7 fusion.44
  10.1 1.2 convert_reduce_fusion
  11.3 1.3 fusion.34
  13.6 0.7 and_reduce_fusion
  14.3 0.7 multiply_reduce_fusion.3
  15.1 15.5 %scatter_custom_fusion.2 = s32[512]{0:T(512)S(1)} fusion(s32[4096]{0:T(1024)S(1)} %bitcast.77, s32[4096]{0:T(1024)S(1)} %bitcast.76, s32[]{:T(128)} %constant.24.clone.1), kind=kCustom, calls=%fused_computation.82 | custom fusion | bytes 2052
  30.8 1.3 fusion.27
  32.2 2.1 gather_fusion.2
  34.2 32.0 %all_to_all.37 = bf16[16,32,1024]{2,1,0:T(8,128)(2,1)} all-to-all(bf16[16,32,1024]{2,1,0:T(8,128)(2,1)S(1)} %bitcast.69), channel_id=1, replica_groups=mesh['dp'=2,'expert'=16] {'expert'}, dimensions={0} | all-to-all | bytes 2097152 | tf_op jit(solution)/shard_map/all_to_all | solution.py:91
  66.4 2.1 gather_fusion.1
  68.4 29.6 %all_to_all.38 = bf16[16,32,1024]{2,1,0:T(8,128)(2,1)} all-to-all(bf16[16,32,1024]{2,1,0:T(8,128)(2,1)S(1)} %bitcast.68), channel_id=1, replica_groups=mesh['dp'=2,'expert'=16] {'expert'}, dimensions={0} | all-to-all | bytes 2097152 | tf_op jit(solution)/shard_map/all_to_all | solution.py:92
  98.5 4.9 %gather_fusion = bf16[512]{0:T(512)(128)(2,1)S(1)} fusion(bf16[257,16]{0,1:T(8,128)(2,1)S(1)} %concatenate.23, s32[512]{0:T(512)S(1)} %reshape.169), kind=kCustom, calls=%fused_computation | custom fusion | bytes 6144 | tf_op jit(solution)/shard_map/gather | solution.py:89
  103.5 11.3 %all_to_all.39 = bf16[16,1,32]{2,1,0:T(2,128)(2,1)S(1)} all-to-all(bf16[16,1,32]{2,1,0:T(2,128)(2,1)S(1)} %all_to_all.31), channel_id=1, replica_groups=mesh['dp'=2,'expert'=16] {'expert'}, dimensions={0} | all-to-all | bytes 2048 | tf_op jit(solution)/shard_map/all_to_all | solution.py:93
  114.8 4.7 %all-gather = bf16[32,1,32]{2,0,1:T(8,128)(2,1)S(1)} all-gather(bf16[16,1,32]{2,0,1:T(8,128)(2,1)S(1)} %copy.27), channel_id=2, replica_groups=mesh['dp'=2,'expert'=16] {'dp'}, dimensions={0}, use_global_device_ids=true | all-gather | bytes 3072 | tf_op jit(solution)/shard_map/all_gather | solution.py:98
  119.6 10.5 %fusion.9 = f32[1024,2048]{1,0:T(8,128)} fusion(bf16[1024,1024]{1,0:T(8,128)(2,1)} %bitcast.80, bf16[1,1024,2048]{2,1,0:T(8,128)(2,1)} %param.10), kind=kOutput, calls=%fused_computation.19 | convolution fusion | flops 4294967296 | bytes 14680064 | tf_op jit(solution)/shard_map/dot_general | solution.py:105
  130.1 4.5 %all-gather.4.cloned.1.call-done = bf16[32,32,1024]{2,1,0:T(8,128)(2,1)} async-done(((bf16[16,32,1024]{2,1,0:T(8,128)(2,1)}), bf16[32,32,1024]{2,1,0:T(8,128)(2,1)}) %all-gather.4.cloned.1.call-update) | async-done | bytes 2097168 | tf_op jit(solution)/shard_map/all_gather | solution.py:97
  134.6 14.5 %multiply_reduce_fusion = (f32[1024]{0:T(1024)S(1)}, bf16[1024,2048]{1,0:T(8,128)(2,1)}) fusion(f32[1024,2048]{1,0:T(8,128)} %fusion.9, f32[1024]{0:T(1024)S(1)} %reshape.167, bf16[1024,1024]{1,0:T(8,128)(2,1)} %bitcast.82, bf16[1,2048,1024]{2,1,0:T(8,128)(2,1)} %param.11), kind=kOutput, calls=%fused_computation.15 | convolution fusion | flops 4347395072 | bytes 18882560 | tf_op jit(solution)/shard_map/dot_general | solution.py:106
  149.1 0.7 reshape.160
  149.9 10.0 %fusion.7 = f32[32,32,1024]{2,1,0:T(8,128)} fusion(bf16[32,32,2048]{2,1,0:T(8,128)(2,1)} %bitcast.84, bf16[1,1024,2048]{2,1,0:T(8,128)(2,1)} %param.10), kind=kOutput, calls=%fused_computation.17 | convolution fusion | flops 4294967296 | bytes 12582912 | tf_op jit(solution)/shard_map/dot_general | solution.py:116
  160.0 0.8 subtract_multiply_fusion
  161.4 4.9 %psum.7 = f32[1024,1]{0,1:T(1,128)S(1)} all-reduce(f32[1024,1]{0,1:T(1,128)S(1)} %bitcast.75), channel_id=1, replica_groups=mesh['dp'=2,'expert'=16] {'dp'}, use_global_device_ids=true, to_apply=%region_15.16 | all-reduce | flops 1024 | bytes 8192 | tf_op jit(solution)/shard_map/psum | solution.py:132
  166.3 4.4 %collective-permute-start.8 = (f32[1024,1]{0,1:T(1,128)S(1)}, f32[1024,1]{0,1:T(1,128)S(1)}, u32[]{:S(2)}, u32[]{:S(2)}) collective-permute-start(f32[1024,1]{0,1:T(1,128)S(1)} %psum.7), channel_id=1, source_target_pairs={{0,15},{1,0},{2,1},{3,2},{4,3},{5,4},{6,5},{7,6},{8,7},{9,8},{10,9... | collective-permute-start | bytes 12296 | tf_op jit(solution)/shard_map/ppermute | solution.py:22
  170.8 1.3 collective-permute-done
  172.1 4.4 %collective-permute-start.9 = (f32[1024,1]{0,1:T(1,128)S(1)}, f32[1024,1]{0,1:T(1,128)S(1)}, u32[]{:S(2)}, u32[]{:S(2)}) collective-permute-start(f32[1024,1]{0,1:T(1,128)S(1)} %collective-permute-done.8), channel_id=1, source_target_pairs={{0,15},{1,0},{2,1},{3,2},{4,3},{5,4},{6,5},{7,6},{8,7},{9,8},{10,9... | collective-permute-start | bytes 12296 | tf_op jit(solution)/shard_map/ppermute | solution.py:22
  176.5 1.3 collective-permute-done.1
  177.9 4.4 %collective-permute-start.10 = (f32[1024,1]{0,1:T(1,128)S(1)}, f32[1024,1]{0,1:T(1,128)S(1)}, u32[]{:S(2)}, u32[]{:S(2)}) collective-permute-start(f32[1024,1]{0,1:T(1,128)S(1)} %collective-permute-done.9), channel_id=1, source_target_pairs={{0,15},{1,0},{2,1},{3,2},{4,3},{5,4},{6,5},{7,6},{8,7},{9,8},{10,9... | collective-permute-start | bytes 12296 | tf_op jit(solution)/shard_map/ppermute | solution.py:22
  182.3 1.3 collective-permute-done.2
  183.6 4.4 %collective-permute-start.11 = (f32[1024,1]{0,1:T(1,128)S(1)}, f32[1024,1]{0,1:T(1,128)S(1)}, u32[]{:S(2)}, u32[]{:S(2)}) collective-permute-start(f32[1024,1]{0,1:T(1,128)S(1)} %collective-permute-done.10), channel_id=1, source_target_pairs={{0,15},{1,0},{2,1},{3,2},{4,3},{5,4},{6,5},{7,6},{8,7},{9,8},{10,9... | collective-permute-start | bytes 12296 | tf_op jit(solution)/shard_map/ppermute | solution.py:22
  188.0 1.3 collective-permute-done.3
  189.3 0.6 copy.28
  189.9 5.8 %all-to-all-start.4 = ((bf16[16,1,32]{2,1,0:T(2,128)(2,1)}), bf16[16,1,32]{2,1,0:T(2,128)(2,1)S(1)}, u32[]{:S(2)}, u32[]{:S(2)}) async-start(bf16[16,1,32]{2,1,0:T(2,128)(2,1)} %copy.28), calls=%async_computation.6 | async-start | bytes 16384 | tf_op jit(solution)/shard_map/all_to_all | solution.py:136
  195.9 4.3 %collective-permute-start.12 = (f32[1024,1]{0,1:T(1,128)S(1)}, f32[1024,1]{0,1:T(1,128)S(1)}, u32[]{:S(2)}, u32[]{:S(2)}) collective-permute-start(f32[1024,1]{0,1:T(1,128)S(1)} %collective-permute-done.11), channel_id=1, source_target_pairs={{0,15},{1,0},{2,1},{3,2},{4,3},{5,4},{6,5},{7,6},{8,7},{9,8},{10,9... | collective-permute-start | bytes 12296 | tf_op jit(solution)/shard_map/ppermute | solution.py:22
  200.2 16.8 %reduce-scatter.3.cloned.1.call-done = f32[16,32,1024]{2,1,0:T(8,128)} async-done(((f32[32,32,1024]{2,1,0:T(8,128)}), f32[16,32,1024]{2,1,0:T(8,128)}) %reduce-scatter.3.cloned.1.call-update) | async-done | bytes 2097168 | tf_op jit(solution)/shard_map/reduce_scatter | solution.py:120
  217.1 2.7 convert_element_type.111
  219.8 5.6 %all-to-all-start.3 = ((bf16[16,32,1024]{2,1,0:T(8,128)(2,1)}), bf16[16,32,1024]{2,1,0:T(8,128)(2,1)S(1)}, u32[]{:S(2)}, u32[]{:S(2)}) async-start(bf16[16,32,1024]{2,1,0:T(8,128)(2,1)} %convert_element_type.111), calls=%async_computation.4 | async-start | bytes 2097152 | tf_op jit(solution)/shard_map/all_to_all | solution.py:135
  225.4 12.4 %convert_bitcast_fusion = bf16[1,2048,1024]{2,1,0:T(8,128)(2,1)} fusion(bf16[1024,1024]{1,0:T(8,128)(2,1)} %bitcast.83, f32[1024]{0:T(1024)S(1)} %reshape.167, f32[1024,2048]{1,0:T(8,128)} %fusion.9), kind=kOutput, calls=%fused_computation.23 | convolution fusion | flops 4319084544 | bytes 14684160 | tf_op jit(solution)/shard_map/dot_general | solution.py:113
  237.8 4.3 %collective-permute-start.13 = (f32[1024,1]{0,1:T(1,128)S(1)}, f32[1024,1]{0,1:T(1,128)S(1)}, u32[]{:S(2)}, u32[]{:S(2)}) collective-permute-start(f32[1024,1]{0,1:T(1,128)S(1)} %collective-permute-done.12), channel_id=1, source_target_pairs={{0,15},{1,0},{2,1},{3,2},{4,3},{5,4},{6,5},{7,6},{8,7},{9,8},{10,9... | collective-permute-start | bytes 12296 | tf_op jit(solution)/shard_map/ppermute | solution.py:22
  242.2 6.1 %convert_bitcast_fusion.1 = bf16[1,1024,2048]{2,1,0:T(8,128)(2,1)} fusion(bf16[1024,1024]{1,0:T(8,128)(2,1)S(1)} %bitcast.81, bf16[1024,2048]{1,0:T(8,128)(2,1)S(1)} %copy-done.5), kind=kOutput, calls=%fused_computation.25 | convolution fusion | flops 4297064448 | bytes 10485760 | tf_op jit(solution)/shard_map/dot_general | solution.py:110
  248.3 4.4 %collective-permute-start.14 = (f32[1024,1]{0,1:T(1,128)S(1)}, f32[1024,1]{0,1:T(1,128)S(1)}, u32[]{:S(2)}, u32[]{:S(2)}) collective-permute-start(f32[1024,1]{0,1:T(1,128)S(1)} %collective-permute-done.13), channel_id=1, source_target_pairs={{0,15},{1,0},{2,1},{3,2},{4,3},{5,4},{6,5},{7,6},{8,7},{9,8},{10,9... | collective-permute-start | bytes 12296 | tf_op jit(solution)/shard_map/ppermute | solution.py:22
  252.8 25.9 %scatter_fusion = f32[257,16]{0,1:T(8,128)S(1)} fusion(f32[257,16]{0,1:T(8,128)S(1)} %broadcast_in_dim.30, s32[512]{0:T(512)S(1)} %reshape.199, f32[512]{0:T(512)S(1)} %reshape.201), kind=kCustom, calls=%fused_computation.4 | custom fusion | flops 512 | bytes 10240 | tf_op jit(solution)/shard_map/scatter-add | solution.py:148
  279.0 0.6 constant_dynamic-slice_fusion
  279.7 5.1 %scatter_custom_fusion = f32[257,1024]{1,0:T(8,128)S(1)} fusion(s32[512]{0:T(512)S(1)} %reshape.193, bf16[512,1024]{1,0:T(8,128)(2,1)S(1)} %bitcast.67, f32[]{:T(128)} %constant.23.clone.1), kind=kCustom, calls=%fused_computation.26 | custom fusion | flops 1048576 | bytes 2101252 | tf_op jit(solution)/shard_map/scatter-add | solution.py:141
  284.7 1.1 fusion.33
  285.9 0.6 maximum_bitcast_fusion
  286.5 1.3 fusion.32
  (81 shorter events, 3.4 us)
Async XLA Ops:
  7.2 91.0 %copy-start = (bf16[1024,16]{0,1:T(8,128)(2,1)S(1)}, bf16[1024,16]{0,1:T(8,128)(2,1)}, u32[]{:S(2)}) copy-start(bf16[1024,16]{0,1:T(8,128)(2,1)} %param.9) | copy-start | bytes 98308
  7.2 112.4 %all-gather.6.cloned.1.call-start = ((), (), s32[]{:S(2)}) async-start(), calls=%async_computation.8 | async-start | bytes 3145728 | tf_op jit(solution)/shard_map/all_gather | solution.py:96
  32.1 34.2 %copy-start.3 = (bf16[256,1024]{1,0:T(8,128)(2,1)S(1)}, bf16[256,1024]{1,0:T(8,128)(2,1)}, u32[]{:S(2)}) copy-start(bf16[256,1024]{1,0:T(8,128)(2,1)} %param.13) | copy-start | bytes 1572868
  66.3 68.4 %all-gather.4.cloned.1.call-start = ((), (), s32[]{:S(2)}) async-start(), calls=%async_computation.7 | async-start | bytes 3145728 | tf_op jit(solution)/shard_map/all_gather | solution.py:97
  98.1 61.9 %reduce-scatter.5.cloned.1.call-start = ((), (), s32[]{:S(2)}) async-start(), calls=%async_computation.10 | async-start | bytes 24576 | tf_op jit(solution)/shard_map/reduce_scatter | solution.py:123
  149.8 67.2 %reduce-scatter.3.cloned.1.call-start = ((), (), s32[]{:S(2)}) async-start(), calls=%async_computation.9 | async-start | bytes 6291456 | tf_op jit(solution)/shard_map/reduce_scatter | solution.py:120
  159.9 1.2 copy-start.1
  166.3 5.7 %collective-permute-start = (f32[1024,1]{0,1:T(1,128)S(1)}, f32[1024,1]{0,1:T(1,128)S(1)}, u32[]{:S(2)}, u32[]{:S(2)}) collective-permute-start(f32[1024,1]{0,1:T(1,128)S(1)} %psum.7), channel_id=1, source_target_pairs={{0,1},{1,2},{2,3},{3,4},{4,5},{5,6},{6,7},{7,8},{8,9},{9,10},{10,1... | collective-permute-start | bytes 12296 | tf_op jit(solution)/shard_map/ppermute | solution.py:19
  166.3 5.8 %collective-permute-start.8 = (f32[1024,1]{0,1:T(1,128)S(1)}, f32[1024,1]{0,1:T(1,128)S(1)}, u32[]{:S(2)}, u32[]{:S(2)}) collective-permute-start(f32[1024,1]{0,1:T(1,128)S(1)} %psum.7), channel_id=1, source_target_pairs={{0,15},{1,0},{2,1},{3,2},{4,3},{5,4},{6,5},{7,6},{8,7},{9,8},{10,9... | collective-permute-start | bytes 12296 | tf_op jit(solution)/shard_map/ppermute | solution.py:22
  172.1 5.7 %collective-permute-start.1 = (f32[1024,1]{0,1:T(1,128)S(1)}, f32[1024,1]{0,1:T(1,128)S(1)}, u32[]{:S(2)}, u32[]{:S(2)}) collective-permute-start(f32[1024,1]{0,1:T(1,128)S(1)} %collective-permute-done), channel_id=1, source_target_pairs={{0,1},{1,2},{2,3},{3,4},{4,5},{5,6},{6,7},{7,8},{8,9},{9,10},{10,1... | collective-permute-start | bytes 12296 | tf_op jit(solution)/shard_map/ppermute | solution.py:19
  172.1 5.7 %collective-permute-start.9 = (f32[1024,1]{0,1:T(1,128)S(1)}, f32[1024,1]{0,1:T(1,128)S(1)}, u32[]{:S(2)}, u32[]{:S(2)}) collective-permute-start(f32[1024,1]{0,1:T(1,128)S(1)} %collective-permute-done.8), channel_id=1, source_target_pairs={{0,15},{1,0},{2,1},{3,2},{4,3},{5,4},{6,5},{7,6},{8,7},{9,8},{10,9... | collective-permute-start | bytes 12296 | tf_op jit(solution)/shard_map/ppermute | solution.py:22
  177.8 5.7 %collective-permute-start.2 = (f32[1024,1]{0,1:T(1,128)S(1)}, f32[1024,1]{0,1:T(1,128)S(1)}, u32[]{:S(2)}, u32[]{:S(2)}) collective-permute-start(f32[1024,1]{0,1:T(1,128)S(1)} %collective-permute-done.1), channel_id=1, source_target_pairs={{0,1},{1,2},{2,3},{3,4},{4,5},{5,6},{6,7},{7,8},{8,9},{9,10},{10,1... | collective-permute-start | bytes 12296 | tf_op jit(solution)/shard_map/ppermute | solution.py:19
  177.9 5.7 %collective-permute-start.10 = (f32[1024,1]{0,1:T(1,128)S(1)}, f32[1024,1]{0,1:T(1,128)S(1)}, u32[]{:S(2)}, u32[]{:S(2)}) collective-permute-start(f32[1024,1]{0,1:T(1,128)S(1)} %collective-permute-done.9), channel_id=1, source_target_pairs={{0,15},{1,0},{2,1},{3,2},{4,3},{5,4},{6,5},{7,6},{8,7},{9,8},{10,9... | collective-permute-start | bytes 12296 | tf_op jit(solution)/shard_map/ppermute | solution.py:22
  183.5 5.7 %collective-permute-start.3 = (f32[1024,1]{0,1:T(1,128)S(1)}, f32[1024,1]{0,1:T(1,128)S(1)}, u32[]{:S(2)}, u32[]{:S(2)}) collective-permute-start(f32[1024,1]{0,1:T(1,128)S(1)} %collective-permute-done.2), channel_id=1, source_target_pairs={{0,1},{1,2},{2,3},{3,4},{4,5},{5,6},{6,7},{7,8},{8,9},{9,10},{10,1... | collective-permute-start | bytes 12296 | tf_op jit(solution)/shard_map/ppermute | solution.py:19
  183.6 12.3 %collective-permute-start.11 = (f32[1024,1]{0,1:T(1,128)S(1)}, f32[1024,1]{0,1:T(1,128)S(1)}, u32[]{:S(2)}, u32[]{:S(2)}) collective-permute-start(f32[1024,1]{0,1:T(1,128)S(1)} %collective-permute-done.10), channel_id=1, source_target_pairs={{0,15},{1,0},{2,1},{3,2},{4,3},{5,4},{6,5},{7,6},{8,7},{9,8},{10,9... | collective-permute-start | bytes 12296 | tf_op jit(solution)/shard_map/ppermute | solution.py:22
  189.3 10.9 %collective-permute-start.4 = (f32[1024,1]{0,1:T(1,128)S(1)}, f32[1024,1]{0,1:T(1,128)S(1)}, u32[]{:S(2)}, u32[]{:S(2)}) collective-permute-start(f32[1024,1]{0,1:T(1,128)S(1)} %collective-permute-done.3), channel_id=1, source_target_pairs={{0,1},{1,2},{2,3},{3,4},{4,5},{5,6},{6,7},{7,8},{8,9},{9,10},{10,1... | collective-permute-start | bytes 12296 | tf_op jit(solution)/shard_map/ppermute | solution.py:19
  189.9 29.9 %all-to-all-start.4 = ((bf16[16,1,32]{2,1,0:T(2,128)(2,1)}), bf16[16,1,32]{2,1,0:T(2,128)(2,1)S(1)}, u32[]{:S(2)}, u32[]{:S(2)}) async-start(bf16[16,1,32]{2,1,0:T(2,128)(2,1)} %copy.28), calls=%async_computation.6 | async-start | bytes 16384 | tf_op jit(solution)/shard_map/all_to_all | solution.py:136
  195.9 41.9 %collective-permute-start.12 = (f32[1024,1]{0,1:T(1,128)S(1)}, f32[1024,1]{0,1:T(1,128)S(1)}, u32[]{:S(2)}, u32[]{:S(2)}) collective-permute-start(f32[1024,1]{0,1:T(1,128)S(1)} %collective-permute-done.11), channel_id=1, source_target_pairs={{0,15},{1,0},{2,1},{3,2},{4,3},{5,4},{6,5},{7,6},{8,7},{9,8},{10,9... | collective-permute-start | bytes 12296 | tf_op jit(solution)/shard_map/ppermute | solution.py:22
  200.2 41.9 %collective-permute-start.5 = (f32[1024,1]{0,1:T(1,128)S(1)}, f32[1024,1]{0,1:T(1,128)S(1)}, u32[]{:S(2)}, u32[]{:S(2)}) collective-permute-start(f32[1024,1]{0,1:T(1,128)S(1)} %collective-permute-done.4), channel_id=1, source_target_pairs={{0,1},{1,2},{2,3},{3,4},{4,5},{5,6},{6,7},{7,8},{8,9},{9,10},{10,1... | collective-permute-start | bytes 12296 | tf_op jit(solution)/shard_map/ppermute | solution.py:19
  219.8 59.9 %all-to-all-start.3 = ((bf16[16,32,1024]{2,1,0:T(8,128)(2,1)}), bf16[16,32,1024]{2,1,0:T(8,128)(2,1)S(1)}, u32[]{:S(2)}, u32[]{:S(2)}) async-start(bf16[16,32,1024]{2,1,0:T(8,128)(2,1)} %convert_element_type.111), calls=%async_computation.4 | async-start | bytes 2097152 | tf_op jit(solution)/shard_map/all_to_all | solution.py:135
  225.4 16.7 %copy-start.4 = (bf16[32,32,1024]{2,1,0:T(8,128)(2,1)S(1)}, bf16[32,32,1024]{2,1,0:T(8,128)(2,1)}, u32[]{:S(2)}) copy-start(bf16[32,32,1024]{2,1,0:T(8,128)(2,1)} %all-gather.6.cloned.1.call-done) | copy-start | bytes 6291460
  225.4 16.7 %copy-start.5 = (bf16[1024,2048]{1,0:T(8,128)(2,1)S(1)}, bf16[1024,2048]{1,0:T(8,128)(2,1)}, u32[]{:S(2)}) copy-start(bf16[1024,2048]{1,0:T(8,128)(2,1)} %get-tuple-element.12) | copy-start | bytes 12582916
  237.8 10.5 %collective-permute-start.13 = (f32[1024,1]{0,1:T(1,128)S(1)}, f32[1024,1]{0,1:T(1,128)S(1)}, u32[]{:S(2)}, u32[]{:S(2)}) collective-permute-start(f32[1024,1]{0,1:T(1,128)S(1)} %collective-permute-done.12), channel_id=1, source_target_pairs={{0,15},{1,0},{2,1},{3,2},{4,3},{5,4},{6,5},{7,6},{8,7},{9,8},{10,9... | collective-permute-start | bytes 12296 | tf_op jit(solution)/shard_map/ppermute | solution.py:22
  242.2 10.6 %collective-permute-start.6 = (f32[1024,1]{0,1:T(1,128)S(1)}, f32[1024,1]{0,1:T(1,128)S(1)}, u32[]{:S(2)}, u32[]{:S(2)}) collective-permute-start(f32[1024,1]{0,1:T(1,128)S(1)} %collective-permute-done.5), channel_id=1, source_target_pairs={{0,1},{1,2},{2,3},{3,4},{4,5},{5,6},{6,7},{7,8},{8,9},{9,10},{10,1... | collective-permute-start | bytes 12296 | tf_op jit(solution)/shard_map/ppermute | solution.py:19
  248.3 30.4 %collective-permute-start.14 = (f32[1024,1]{0,1:T(1,128)S(1)}, f32[1024,1]{0,1:T(1,128)S(1)}, u32[]{:S(2)}, u32[]{:S(2)}) collective-permute-start(f32[1024,1]{0,1:T(1,128)S(1)} %collective-permute-done.13), channel_id=1, source_target_pairs={{0,15},{1,0},{2,1},{3,2},{4,3},{5,4},{6,5},{7,6},{8,7},{9,8},{10,9... | collective-permute-start | bytes 12296 | tf_op jit(solution)/shard_map/ppermute | solution.py:22
  252.7 26.0 %collective-permute-start.7 = (f32[1024,1]{0,1:T(1,128)S(1)}, f32[1024,1]{0,1:T(1,128)S(1)}, u32[]{:S(2)}, u32[]{:S(2)}) collective-permute-start(f32[1024,1]{0,1:T(1,128)S(1)} %collective-permute-done.6), channel_id=1, source_target_pairs={{0,1},{1,2},{2,3},{3,4},{4,5},{5,6},{6,7},{7,8},{8,9},{9,10},{10,1... | collective-permute-start | bytes 12296 | tf_op jit(solution)/shard_map/ppermute | solution.py:19
  252.8 31.9 %copy-start.2 = (bf16[256,1024]{1,0:T(8,128)(2,1)S(1)}, bf16[256,1024]{1,0:T(8,128)(2,1)}, u32[]{:S(2)}) copy-start(bf16[256,1024]{1,0:T(8,128)(2,1)} %param.7) | copy-start | bytes 1572868
Sparse Core Ops, SparseCore 0:
  66.4 33.4 all-gather.5
  101.4 33.1 all-gather.3
  149.9 9.9 reduce-scatter.4
  162.6 54.3 reduce-scatter.2
